TPU v7x, 512 devices: a whole 4x8x8 slice. The times are simulated.
512 devices in a mesh: grp: 16 (over y, core), ops: 32 (over x, z).
Axes of the slice: x: 4, y: 8, z: 8, core: 2. Of those that a mesh axis runs over, the one named last changes fastest.
Arguments:
- op_embed: bfloat16 [131072, 256], P(('grp', 'ops')), may hold values from -6 to 6
- machine_embed: bfloat16 [8192, 256], P('grp'), may hold values from -6 to 6
- cotangent: bfloat16 [131072, 256], P(('grp', 'ops')), may hold values from -6 to 6
- w_query: bfloat16 [256, 256], replicated, may hold values from -0.375 to 0.375
- w_key: bfloat16 [256, 256], replicated, may hold values from -0.375 to 0.375
- w_value: bfloat16 [256, 256], replicated, may hold values from -0.375 to 0.375
- slot_local: int32 [512, 16], P(('grp', 'ops')), may hold values from 0 to 3
- counts: int32 [131072, 16], P(('grp', 'ops')), may hold values from 0 to 128, as said below
Outputs:
- op_grad: bfloat16 [131072, 256], P(('grp', 'ops'))
- machine_grad: float32 [8192, 256], P(('grp', 'ops'))
- grad_wq: float32 [256, 256], replicated
- grad_wk: float32 [256, 256], replicated
- grad_wv: float32 [256, 256], replicated
Inputs may be any that keep to these rules, and one draw needn't show every extreme that they name: The eligible machines of slot e's block for operation o are its first counts[o, e] machines; 0 means the operation has no eligible machine in that block.
All inputs are finite; a program needn't handle non-finite values.
Results may differ from a plain program's by a relative error of at most 0.0056.
Values may be sent and summed in bfloat16 or wider, within the bound.
No kernel may reach another device: no remote copies, remote signals or barrier semaphores. Data moves between devices by JAX's collectives and lax.ppermute only.
A program may use at most 64 MiB of HBM per device.

v0:
```python
import jax
import jax.numpy as jnp
from jax import lax
from jax.sharding import PartitionSpec as P

HEADS = 8
BLK = 128
mean_scale = 0.08838834764831845


def slot_grads(queries, cotangent4, key_rows, value_rows, lengths):
    head_size = queries.shape[2]
    inv_root = head_size ** (-0.5)
    scores = (
        jnp.einsum("ohc,mhc->ohm", queries, key_rows, preferred_element_type=jnp.float32) * inv_root
    )
    sigmoid_score = jax.nn.sigmoid(scores)
    columns = lax.broadcasted_iota(jnp.int32, scores.shape, 2)
    eligible = columns < lengths[:, None, None]
    gates = jnp.where(eligible, sigmoid_score, 0.0).astype(jnp.bfloat16)
    value_dot = jnp.einsum(
        "ohc,mhc->ohm", cotangent4, value_rows, preferred_element_type=jnp.float32
    )
    dscore = jnp.where(
        eligible, mean_scale * value_dot * sigmoid_score * (1.0 - sigmoid_score) * inv_root, 0.0
    ).astype(jnp.bfloat16)
    query_part = jnp.einsum("ohm,mhc->ohc", dscore, key_rows, preferred_element_type=jnp.float32)
    key_grad = jnp.einsum(
        "ohm,ohc->mhc", dscore, queries, preferred_element_type=jnp.float32
    ).astype(jnp.bfloat16)
    value_grad = (
        mean_scale
        * jnp.einsum("ohm,ohc->mhc", gates, cotangent4, preferred_element_type=jnp.float32)
    ).astype(jnp.bfloat16)
    return (query_part, key_grad, value_grad)


def per_device(op_embed, machine_embed, cotangent, w_query, w_key, w_value, slot_local, counts):
    groups = lax.axis_size("grp")
    ops_count = op_embed.shape[0]
    model_width = op_embed.shape[1]
    head_size = model_width // HEADS
    machine_rows = machine_embed.shape[0]
    blocks_here = machine_rows // BLK
    highest = lax.Precision.HIGHEST
    both_weights = jnp.concatenate([w_key, w_value], axis=1)
    queries = jnp.dot(op_embed, w_query, preferred_element_type=jnp.float32).astype(jnp.bfloat16)
    wanted = lax.all_to_all(
        slot_local.reshape(groups, 1), "grp", split_axis=0, concat_axis=0, tiled=True
    )
    wanted_ids = wanted[:, 0]
    picker = wanted_ids[:, None] == jnp.arange(blocks_here, dtype=jnp.int32)[None, :]
    local_pairs = jnp.dot(machine_embed, both_weights, preferred_element_type=jnp.float32).astype(
        jnp.bfloat16
    )
    outgoing = local_pairs.reshape(blocks_here, BLK, 2 * model_width)[wanted_ids]
    fetched = lax.all_to_all(outgoing, "grp", split_axis=0, concat_axis=0, tiled=True)
    key_slots = fetched[:, :, :model_width].reshape(groups, BLK, HEADS, head_size)
    value_slots = fetched[:, :, model_width:].reshape(groups, BLK, HEADS, head_size)
    query_heads = queries.reshape(ops_count, HEADS, head_size)
    cot_heads = cotangent.reshape(ops_count, HEADS, head_size)

    def per_slot(summed_q, pieces):
        key_rows, value_rows, lengths = pieces
        query_part, key_grad, value_grad = slot_grads(
            query_heads, cot_heads, key_rows, value_rows, lengths
        )
        return (
            summed_q + query_part,
            (key_grad.reshape(BLK, model_width), value_grad.reshape(BLK, model_width)),
        )

    start_q = jnp.zeros((ops_count, HEADS, head_size), jnp.float32)
    summed_q, (key_grads, value_grads) = lax.scan(
        per_slot, start_q, (key_slots, value_slots, counts.T)
    )
    grad_query = summed_q.astype(jnp.bfloat16).reshape(ops_count, model_width)
    op_grad = (
        cotangent.astype(jnp.float32)
        + jnp.dot(grad_query, w_query.T, preferred_element_type=jnp.float32)
    ).astype(jnp.bfloat16)
    wq_term = jnp.einsum("od,oe->de", op_embed, grad_query, preferred_element_type=jnp.float32)
    returned = lax.all_to_all(
        jnp.concatenate([key_grads, value_grads], axis=2),
        "grp",
        split_axis=0,
        concat_axis=0,
        tiled=True,
    )
    summed = jnp.einsum(
        "gb,gr->br",
        picker.astype(jnp.bfloat16),
        returned.reshape(groups, BLK * 2 * model_width),
        preferred_element_type=jnp.float32,
    )
    summed = summed.reshape(machine_rows, 2 * model_width)
    key_total = summed[:, :model_width]
    value_total = summed[:, model_width:]
    machine_part = jnp.dot(key_total, w_key.astype(jnp.float32).T, precision=highest) + jnp.dot(
        value_total, w_value.astype(jnp.float32).T, precision=highest
    )
    embed_f = machine_embed.astype(jnp.float32)
    wk_term = jnp.dot(embed_f.T, key_total, precision=highest)
    wv_term = jnp.dot(embed_f.T, value_total, precision=highest)
    summed_total = lax.psum(machine_part, "ops")
    share_rows = machine_rows // lax.axis_size("ops")
    first_row = lax.axis_index("ops") * share_rows
    machine_grad = lax.dynamic_slice_in_dim(summed_total, first_row, share_rows, 0)
    weight_sums = lax.psum((wq_term, wk_term, wv_term), ("grp", "ops"))
    shard_count = float(groups * lax.axis_size("ops"))
    grad_wq = weight_sums[0] / shard_count
    grad_wk = weight_sums[1] / shard_count
    grad_wv = weight_sums[2] / shard_count
    return (op_grad, machine_grad, grad_wq, grad_wk, grad_wv)


def solution(mesh):
    return jax.shard_map(
        per_device,
        mesh=mesh,
        in_specs=(
            P(("grp", "ops"), None),
            P("grp", None),
            P(("grp", "ops"), None),
            P(),
            P(),
            P(),
            P(("grp", "ops"), None),
            P(("grp", "ops"), None),
        ),
        out_specs=(P(("grp", "ops"), None), P(("grp", "ops"), None), P(), P(), P()),
        check_vma=False,
    )
```

profile of v0, /device:TPU:8, one launch (start us, length us, event | category | flops | bytes accessed | tf_op | source)
XLA Modules:
  0.0 657.2 jit_solution(9235457132968034616)
XLA Ops:
  7.2 1.4 copy.46
  8.6 9.1 %all-to-all-start = ((s32[16,1,1]{2,1,0:T(1,128)}), s32[16,1,1]{2,1,0:T(1,128)S(1)}, u32[]{:S(2)}, u32[]{:S(2)}) async-start(s32[16,1,1]{2,1,0:T(1,128)} %copy.46), calls=%async_computation | async-start | bytes 16384 | tf_op jit(solution)/shard_map/all_to_all | solution.py:48
  17.6 1.3 convolution_convert_fusion.1
  18.9 4.9 all-to-all-done
  24.2 2.0 gather_fusion
  26.2 5.1 all-to-all-start.1
  31.7 46.8 %all-to-all-done.1 = bf16[16,128,512]{2,1,0:T(8,128)(2,1)S(1)} async-done(((bf16[16,128,512]{2,1,0:T(8,128)(2,1)}), bf16[16,128,512]{2,1,0:T(8,128)(2,1)S(1)}, u32[]{:S(2)}, u32[]{:S(2)}) %all-to-all-start.1) | async-done | bytes 2097184 | tf_op jit(solution)/shard_map/all_to_all | solution.py:57
  78.6 1.6 fusion.38
  80.2 1.7 copy.47
  81.9 1.3 copy.48
  83.2 63.6 %while.15 = (s32[]{:T(128)}, f32[256,8,32]{0,2,1:T(8,128)S(1)}, bf16[16,128,256]{1,2,0:T(8,128)(2,1)}, bf16[16,128,256]{1,2,0:T(8,128)(2,1)}, bf16[16,128,8,32]{...) while((s32[]{:T(128)}, f32[256,8,32]{0,2,1:T(8,128)S(1)}, ...), condition=%wide.region_1.2_spmd.clone, body=%wide.region_0.1_spmd.clone.sunk | while | flops 87785472 | bytes 6361235 | solution.py:74
  84.4 1.3 fusion.80
  87.7 0.7 constant_dynamic-slice_fusion.3
  88.4 1.3 fusion.80
  91.7 0.7 constant_dynamic-slice_fusion.3
  92.4 1.3 fusion.80
  95.6 0.7 constant_dynamic-slice_fusion.3
  96.3 1.3 fusion.80
  100.3 1.3 fusion.80
  104.3 1.3 fusion.80
  108.2 1.3 fusion.80
  112.2 1.3 fusion.80
  116.2 1.3 fusion.80
  120.2 1.3 fusion.80
  124.1 1.3 fusion.80
  128.1 1.3 fusion.80
  132.1 1.3 fusion.80
  136.1 1.3 fusion.80
  140.1 1.3 fusion.80
  144.0 1.3 fusion.80
  146.8 3.1 pad_maximum_fusion
  149.9 6.9 %all-to-all-start.2 = ((bf16[16,128,512]{1,2,0:T(8,128)(2,1)}), bf16[16,128,512]{1,2,0:T(8,128)(2,1)}, u32[]{:S(2)}, u32[]{:S(2)}) async-start(bf16[16,128,512]{1,2,0:T(8,128)(2,1)} %pad_maximum_fusion), calls=%async_computation.2 | async-start | bytes 4194304 | tf_op jit(solution)/shard_map/all_to_all | solution.py:83
  156.8 0.9 convolution_bitcast_fusion.3
  157.7 46.3 %all-to-all-done.2 = bf16[16,128,512]{1,2,0:T(8,128)(2,1)} async-done(((bf16[16,128,512]{1,2,0:T(8,128)(2,1)}), bf16[16,128,512]{1,2,0:T(8,128)(2,1)}, u32[]{:S(2)}, u32[]{:S(2)}) %all-to-all-start.2) | async-done | bytes 2097184 | tf_op jit(solution)/shard_map/all_to_all | solution.py:83
  204.0 3.4 copy.57
  208.0 0.7 reshape.79
  208.7 1.3 convolution_bitcast_fusion.2
  210.0 1.3 convolution_bitcast_fusion.1
  211.9 1.2 convolution_add_fusion
  213.1 0.9 fusion.25
  214.0 274.6 %all-reduce.6.cloned.1.call-done = (f32[256,256]{0,1:T(8,128)}, f32[256,256]{0,1:T(8,128)}, f32[256,256]{0,1:T(8,128)}) async-done(((f32[256,256]{0,1:T(8,128)}, f32[256,256]{0,1:T(8,128)}, f32[256,256]{0,1:T(8,128)}), (f32[256,256]{0,1:T(8,128)}, f32[256,256]{0,1:T(8,128)}, f32[256,256]{0,1:T(8,128)})) %all-reduce.6.cloned.1.call-update) | async-done | bytes 786448 | tf_op jit(solution)/shard_map/psum | solution.py:109
  488.6 1.0 broadcast_multiply_fusion.2
  489.6 0.8 copy.51
  490.4 1.1 broadcast_multiply_fusion
  491.5 0.8 copy.52
  492.3 0.8 copy.53
  493.2 155.8 %all-reduce.4.cloned.1.call-done = f32[512,256]{1,0:T(8,128)} async-done(((f32[512,256]{1,0:T(8,128)}), f32[512,256]{1,0:T(8,128)}) %all-reduce.4.cloned.1.call-update) | async-done | bytes 524304 | tf_op jit(solution)/shard_map/psum | solution.py:105
  649.0 1.3 constant_dynamic-slice_fusion.1
  (128 shorter events, 42.0 us)
Async XLA Ops:
  7.2 10.5 %copy-start = (bf16[512,256]{1,0:T(8,128)(2,1)S(1)}, bf16[512,256]{1,0:T(8,128)(2,1)}, u32[]{:S(2)}) copy-start(bf16[512,256]{1,0:T(8,128)(2,1)} %param.11) | copy-start | bytes 786436
  8.6 15.3 %all-to-all-start = ((s32[16,1,1]{2,1,0:T(1,128)}), s32[16,1,1]{2,1,0:T(1,128)S(1)}, u32[]{:S(2)}, u32[]{:S(2)}) async-start(s32[16,1,1]{2,1,0:T(1,128)} %copy.46), calls=%async_computation | async-start | bytes 16384 | tf_op jit(solution)/shard_map/all_to_all | solution.py:48
  26.2 5.1 copy-start.6
  26.2 5.3 copy-start.2
  26.2 5.3 copy-start.4
  26.2 52.3 %all-to-all-start.1 = ((bf16[16,128,512]{2,1,0:T(8,128)(2,1)}), bf16[16,128,512]{2,1,0:T(8,128)(2,1)S(1)}, u32[]{:S(2)}, u32[]{:S(2)}) async-start(bf16[16,128,512]{2,1,0:T(8,128)(2,1)} %gather_fusion), calls=%async_computation.1 | async-start | bytes 4194304 | tf_op jit(solution)/shard_map/all_to_all | solution.py:57
  80.2 1.7 copy-start.1
  149.9 6.9 %copy-start.3 = (bf16[256,256]{1,0:T(8,128)(2,1)S(1)}, bf16[256,256]{1,0:T(8,128)(2,1)}, u32[]{:S(2)}) copy-start(bf16[256,256]{1,0:T(8,128)(2,1)} %param.10) | copy-start | bytes 393220
  149.9 54.2 %all-to-all-start.2 = ((bf16[16,128,512]{1,2,0:T(8,128)(2,1)}), bf16[16,128,512]{1,2,0:T(8,128)(2,1)}, u32[]{:S(2)}, u32[]{:S(2)}) async-start(bf16[16,128,512]{1,2,0:T(8,128)(2,1)} %pad_maximum_fusion), calls=%async_computation.2 | async-start | bytes 4194304 | tf_op jit(solution)/shard_map/all_to_all | solution.py:83
  156.8 331.9 %all-reduce.6.cloned.1.call-start = ((), (), s32[]{:S(2)}) async-start(), calls=%async_computation.4 | async-start | bytes 1572864 | tf_op jit(solution)/shard_map/psum | solution.py:109
  208.0 3.4 copy-start.8
  208.7 3.1 copy-start.9
  211.3 1.8 copy-start.5
  211.3 1.8 copy-start.7
  211.4 437.6 %all-reduce.4.cloned.1.call-start = ((), (), s32[]{:S(2)}) async-start(), calls=%async_computation.3 | async-start | bytes 1048576 | tf_op jit(solution)/shard_map/psum | solution.py:105
Sparse Core Ops, SparseCore 0:
  211.5 277.0 all-reduce.5
  492.0 156.9 all-reduce.3
where the time goes:
time: 659 us; the launch traced here: 657 us
  waiting for transfers between devices  529 us (80%)
  matrix products  48.8 us (7%)
  local copies, waits for them, and re-layouts  38.4 us (6%)
  starting transfers between devices  21.1 us (3%)
  between operations  14.3 us (2%)
    psum x1, waiting for transfers between devices, per_device(): weight_sums = lax.psum((wq_term, wk_term, wv_term), ('grp', 'ops'))  275 us
    psum x1, waiting for transfers between devices, per_device(): summed_total = lax.psum(machine_part, 'ops')  156 us
    all_to_all x1, waiting for transfers between devices, per_device(): lax.all_to_all(outgoing, 'grp', split_axis=0, concat_axis=0, tiled=True)  46.8 us
    all_to_all x1, waiting for transfers between devices, per_device(): lax.all_to_all(jnp.concatenate([key_grads, value_grads], axis=2), 'grp',...  46.3 us
    dot_general x16, matrix products, slot_grads(): jnp.einsum('ohc,mhc->ohm', cotangent4, value_rows, preferred_element_type...  20.9 us
  transfers between devices with their start and end apart: 5, of which 5 were waited for; matrix products, arithmetic and copies ran while one was open for 1% of the time, Pallas kernels for 0%

commit v1 on v0

--- a/solution.py
+++ b/solution.py
@@ -102,7 +102,8 @@
     embed_f = machine_embed.astype(jnp.float32)
     wk_term = jnp.dot(embed_f.T, key_total, precision=highest)
     wv_term = jnp.dot(embed_f.T, value_total, precision=highest)
-    summed_total = lax.psum(machine_part, "ops")
+    parts = lax.all_gather(machine_part, "ops")
+    summed_total = jnp.sum(parts, axis=0)
     share_rows = machine_rows // lax.axis_size("ops")
     first_row = lax.axis_index("ops") * share_rows
     machine_grad = lax.dynamic_slice_in_dim(summed_total, first_row, share_rows, 0)

time: 659 us -> 569 us (0.86)
  the two profiles are of different devices: /device:TPU:8 before, /device:TPU:17 now
where the time goes in v1:
time: 569 us; the launch traced here: 567 us
  waiting for transfers between devices  430 us (76%)
  matrix products  50.5 us (9%)
  local copies, waits for them, and re-layouts  37.2 us (7%)
  starting transfers between devices  22 us (4%)
  between operations  15.7 us (3%)
  other arithmetic  11.5 us (2%)
    psum x1, waiting for transfers between devices, per_device(): weight_sums = lax.psum((wq_term, wk_term, wv_term), ('grp', 'ops'))  332 us
    all_to_all x1, waiting for transfers between devices, per_device(): lax.all_to_all(outgoing, 'grp', split_axis=0, concat_axis=0, tiled=True)  47.1 us
    all_to_all x1, waiting for transfers between devices, per_device(): lax.all_to_all(jnp.concatenate([key_grads, value_grads], axis=2), 'grp',...  46.5 us
    dot_general x16, matrix products, slot_grads(): jnp.einsum('ohc,mhc->ohm', cotangent4, value_rows, preferred_element_type...  20.9 us
  transfers between devices with their start and end apart: 5, of which 4 were waited for; matrix products, arithmetic and copies ran while one was open for 2% of the time, Pallas kernels for 0%

profile of v1, /device:TPU:17, one launch (start us, length us, event | category | flops | bytes accessed | tf_op | source)
XLA Modules:
  0.0 567.1 jit_solution(2654259179481988658)
XLA Ops:
  8.0 1.4 copy.46
  9.4 9.2 %all-to-all-start = ((s32[16,1,1]{2,1,0:T(1,128)}), s32[16,1,1]{2,1,0:T(1,128)S(1)}, u32[]{:S(2)}, u32[]{:S(2)}) async-start(s32[16,1,1]{2,1,0:T(1,128)} %copy.46), calls=%async_computation | async-start | bytes 16384 | tf_op jit(solution)/shard_map/all_to_all | solution.py:48
  18.6 1.3 convolution_convert_fusion.1
  19.9 3.7 all-to-all-done
  24.1 2.0 gather_fusion
  26.1 6.3 %all-to-all-start.1 = ((bf16[16,128,512]{2,1,0:T(8,128)(2,1)}), bf16[16,128,512]{2,1,0:T(8,128)(2,1)S(1)}, u32[]{:S(2)}, u32[]{:S(2)}) async-start(bf16[16,128,512]{2,1,0:T(8,128)(2,1)} %gather_fusion), calls=%async_computation.1 | async-start | bytes 4194304 | tf_op jit(solution)/shard_map/all_to_all | solution.py:57
  32.8 47.1 %all-to-all-done.1 = bf16[16,128,512]{2,1,0:T(8,128)(2,1)S(1)} async-done(((bf16[16,128,512]{2,1,0:T(8,128)(2,1)}), bf16[16,128,512]{2,1,0:T(8,128)(2,1)S(1)}, u32[]{:S(2)}, u32[]{:S(2)}) %all-to-all-start.1) | async-done | bytes 2097184 | tf_op jit(solution)/shard_map/all_to_all | solution.py:57
  79.9 1.6 fusion.38
  81.5 1.7 copy.47
  83.2 1.3 copy.48
  84.5 63.7 %while.15 = (s32[]{:T(128)}, f32[256,8,32]{0,2,1:T(8,128)S(1)}, bf16[16,128,256]{1,2,0:T(8,128)(2,1)}, bf16[16,128,256]{1,2,0:T(8,128)(2,1)}, bf16[16,128,8,32]{...) while((s32[]{:T(128)}, f32[256,8,32]{0,2,1:T(8,128)S(1)}, ...), condition=%wide.region_1.2_spmd.clone, body=%wide.region_0.1_spmd.clone.sunk | while | flops 87785472 | bytes 6362243 | solution.py:74
  85.7 1.3 fusion.80
  89.7 1.3 fusion.80
  93.7 1.3 fusion.80
  97.0 0.7 constant_dynamic-slice_fusion.3
  97.7 1.3 fusion.80
  101.7 1.3 fusion.80
  104.9 0.7 constant_dynamic-slice_fusion.3
  105.6 1.3 fusion.80
  108.9 0.7 constant_dynamic-slice_fusion.3
  109.6 1.3 fusion.80
  113.6 1.3 fusion.80
  117.6 1.3 fusion.80
  120.8 0.7 constant_dynamic-slice_fusion.3
  121.6 1.3 fusion.80
  125.5 1.3 fusion.80
  129.5 1.3 fusion.80
  133.5 1.3 fusion.80
  137.5 1.3 fusion.80
  141.5 1.3 fusion.80
  145.4 1.3 fusion.80
  148.2 3.1 pad_maximum_fusion
  151.3 6.4 %all-to-all-start.2 = ((bf16[16,128,512]{1,2,0:T(8,128)(2,1)}), bf16[16,128,512]{1,2,0:T(8,128)(2,1)S(1)}, u32[]{:S(2)}, u32[]{:S(2)}) async-start(bf16[16,128,512]{1,2,0:T(8,128)(2,1)} %pad_maximum_fusion), calls=%async_computation.2 | async-start | bytes 4194304 | tf_op jit(solution)/shard_map/all_to_all | solution.py:83
  157.8 0.9 convolution_bitcast_fusion.3
  158.7 46.5 %all-to-all-done.2 = bf16[16,128,512]{1,2,0:T(8,128)(2,1)S(1)} async-done(((bf16[16,128,512]{1,2,0:T(8,128)(2,1)}), bf16[16,128,512]{1,2,0:T(8,128)(2,1)S(1)}, u32[]{:S(2)}, u32[]{:S(2)}) %all-to-all-start.2) | async-done | bytes 2097184 | tf_op jit(solution)/shard_map/all_to_all | solution.py:83
  205.2 3.0 copy.57
  208.2 2.2 fusion.34
  210.4 0.7 reshape.79
  211.1 1.3 convolution_bitcast_fusion.1
  212.4 1.3 convolution_bitcast_fusion.2
  214.2 1.2 convolution_add_fusion
  215.5 0.9 fusion.25
  216.3 332.2 %all-reduce.3.cloned.1.call-done = (f32[256,256]{0,1:T(8,128)}, f32[256,256]{0,1:T(8,128)}, f32[256,256]{0,1:T(8,128)}) async-done(((f32[256,256]{0,1:T(8,128)}, f32[256,256]{0,1:T(8,128)}, f32[256,256]{0,1:T(8,128)}), (f32[256,256]{0,1:T(8,128)}, f32[256,256]{0,1:T(8,128)}, f32[256,256]{0,1:T(8,128)})) %all-reduce.3.cloned.1.call-update) | async-done | bytes 786448 | tf_op jit(solution)/shard_map/psum | solution.py:110
  548.5 1.1 broadcast_multiply_fusion
  549.6 0.8 copy.52
  550.4 0.8 copy.53
  551.3 0.8 copy.51
  552.2 6.9 %reduce_sum.9 = f32[512,256]{1,0:T(8,128)S(1)} reduce(f32[32,512,256]{2,1,0:T(8,128)} %bitcast.106, f32[]{:T(128)} %constant.16.clone.1), dimensions={0}, to_apply=%region_2.3 | reduce | flops 4063232 | bytes 17301508 | tf_op jit(solution)/shard_map/reduce_sum | solution.py:106
  (125 shorter events, 41.3 us)
Async XLA Ops:
  8.0 10.6 %copy-start = (bf16[512,256]{1,0:T(8,128)(2,1)S(1)}, bf16[512,256]{1,0:T(8,128)(2,1)}, u32[]{:S(2)}) copy-start(bf16[512,256]{1,0:T(8,128)(2,1)} %param.11) | copy-start | bytes 786436
  9.4 14.3 %all-to-all-start = ((s32[16,1,1]{2,1,0:T(1,128)}), s32[16,1,1]{2,1,0:T(1,128)S(1)}, u32[]{:S(2)}, u32[]{:S(2)}) async-start(s32[16,1,1]{2,1,0:T(1,128)} %copy.46), calls=%async_computation | async-start | bytes 16384 | tf_op jit(solution)/shard_map/all_to_all | solution.py:48
  26.1 6.3 %copy-start.4 = (bf16[256,256]{1,0:T(8,128)(2,1)S(1)}, bf16[256,256]{1,0:T(8,128)(2,1)}, u32[]{:S(2)}) copy-start(bf16[256,256]{1,0:T(8,128)(2,1)} %param.12) | copy-start | bytes 393220
  26.1 6.4 %copy-start.2 = (bf16[256,256]{1,0:T(8,128)(2,1)S(1)}, bf16[256,256]{1,0:T(8,128)(2,1)}, u32[]{:S(2)}) copy-start(bf16[256,256]{1,0:T(8,128)(2,1)} %param.10) | copy-start | bytes 393220
  26.1 6.4 %copy-start.3 = (bf16[256,256]{1,0:T(8,128)(2,1)S(1)}, bf16[256,256]{1,0:T(8,128)(2,1)}, u32[]{:S(2)}) copy-start(bf16[256,256]{1,0:T(8,128)(2,1)} %param.13) | copy-start | bytes 393220
  26.1 53.8 %all-to-all-start.1 = ((bf16[16,128,512]{2,1,0:T(8,128)(2,1)}), bf16[16,128,512]{2,1,0:T(8,128)(2,1)S(1)}, u32[]{:S(2)}, u32[]{:S(2)}) async-start(bf16[16,128,512]{2,1,0:T(8,128)(2,1)} %gather_fusion), calls=%async_computation.1 | async-start | bytes 4194304 | tf_op jit(solution)/shard_map/all_to_all | solution.py:57
  81.5 1.7 copy-start.1
  151.3 53.9 %all-to-all-start.2 = ((bf16[16,128,512]{1,2,0:T(8,128)(2,1)}), bf16[16,128,512]{1,2,0:T(8,128)(2,1)S(1)}, u32[]{:S(2)}, u32[]{:S(2)}) async-start(bf16[16,128,512]{1,2,0:T(8,128)(2,1)} %pad_maximum_fusion), calls=%async_computation.2 | async-start | bytes 4194304 | tf_op jit(solution)/shard_map/all_to_all | solution.py:83
  157.7 390.8 %all-reduce.3.cloned.1.call-start = ((), (), s32[]{:S(2)}) async-start(), calls=%async_computation.4 | async-start | bytes 1572864 | tf_op jit(solution)/shard_map/psum | solution.py:110
  210.3 3.4 copy-start.5
  211.1 3.1 copy-start.6
  213.7 338.4 %all-gather.3.cloned.1.call-start = ((), (), s32[]{:S(2)}) async-start(), calls=%async_computation.3 | async-start | bytes 17301504 | tf_op jit(solution)/shard_map/all_gather | solution.py:105
  548.5 2.8 copy-start.7
Sparse Core Ops, SparseCore 0:
  213.8 334.6 all-reduce.2
Sparse Core Ops, SparseCore 1:
  217.4 147.3 all-gather.2
